TPU v7x, 32 devices: a whole 2x2x4 slice. The times are simulated.
32 devices in a mesh: section: 2 (over core), dp: 4 (over y, x), tensor: 4 (over z).
Axes of the slice: x: 2, y: 2, z: 4, core: 2. Of those that a mesh axis runs over, the one named last changes fastest.
Arguments:
- section_input: bfloat16 [2, 512, 4096], P('section', 'dp'), may hold values from -60 to 60
- weights: bfloat16 [2, 4096, 4096], P('section', 'tensor', 'dp'), may hold values from -0.1875 to 0.1875
- gains: float32 [2, 4096], P('section'), may hold values from 0.1 to 1.9
- proj_seeds: int32 [2, 2], P('section'), may hold values from 0 to 99999
- out_grad: bfloat16 [512, 4096], P('dp'), may hold values from -0.75 to 0.75
- query_grads: bfloat16 [2, 256, 4096], P('section', 'dp', 'tensor'), may hold values from -0.017944336 to 0.017944336
Outputs:
- projected_grads: float32 [2, 2, 4096], P('section', None, 'tensor')
- scores: float32 [2, 256], P(None, 'dp')
All inputs are finite; a program needn't handle non-finite values.
Results may differ from a plain program's by a relative error of at most 0.033.
Values may be sent and summed in bfloat16 or wider, within the bound.
A program may use at most 64 MiB of HBM per device.

v0:
```python
import math
import jax
import jax.numpy as jnp
from jax import lax
from jax.sharding import PartitionSpec as P

R = 64
SEQS = 2
MICRO = 16
eps = 1e-05


def passed_along(value, axis, steps):
    count = lax.axis_size(axis)
    first, last = (max(0, -steps), min(count, count - steps))
    return lax.ppermute(value, axis, [(source, source + steps) for source in range(first, last)])


def sign_table(seed_value, row_count):
    row_index = lax.broadcasted_iota(jnp.int32, (row_count, R), 0)
    col_index = lax.broadcasted_iota(jnp.int32, (row_count, R), 1)
    mixing = row_index * 40503 + col_index * 9973 + seed_value * 7919 + 12345
    mixing = mixing ^ mixing >> 13
    mixing = mixing * 1274126177
    mixing = mixing ^ mixing >> 16
    parity = mixing >> 10 & 1
    return (jnp.where(parity == 1, 1.0, -1.0) * (1.0 / math.sqrt(row_count))).astype(jnp.bfloat16)


def take_rows(table, row_start):
    return lax.dynamic_slice_in_dim(table, row_start, MICRO, 0)


def body(section_input, weights, gains, proj_seeds, out_grad, query_grads):
    section_count = lax.axis_size("section")
    section_index = lax.axis_index("section")
    data_count = lax.axis_size("dp")
    data_index = lax.axis_index("dp")
    split_count = lax.axis_size("tensor")
    split_index = lax.axis_index("tensor")
    tok_rows = section_input.shape[1]
    feature_width = section_input.shape[2]
    slice_width = feature_width // split_count
    blocks = tok_rows // MICRO
    turn_count = section_count + blocks - 1
    own_start = split_index * slice_width
    gain_row = gains[0]
    hidden_in = section_input[0].astype(jnp.float32)
    radius = jnp.sqrt(jnp.mean(hidden_in * hidden_in, axis=1, keepdims=True) + eps)
    normed = hidden_in / radius
    lifted = (normed * gain_row).astype(jnp.bfloat16)
    weight_rows = lax.all_gather(weights[0], "dp", axis=1, tiled=True)
    lifted_own = lax.dynamic_slice_in_dim(lifted, own_start, slice_width, 1)
    partial_value = jnp.dot(lifted_own, weight_rows, preferred_element_type=jnp.float32)
    summed = lax.psum(partial_value.astype(jnp.bfloat16), "tensor").astype(jnp.float32)
    sigmoid_z = jax.nn.sigmoid(summed)
    slopes = sigmoid_z * (1.0 + summed * (1.0 - sigmoid_z))
    proj_in = sign_table(proj_seeds[0, 0], feature_width)
    proj_out = sign_table(proj_seeds[0, 1], feature_width)
    in_features = jnp.dot(lifted, proj_in, preferred_element_type=jnp.float32).astype(jnp.bfloat16)
    chain_depth = section_count - 1 - section_index
    at_top = section_index == section_count - 1

    def block_grad(operands):
        upstream, slope_rows, feature_rows, grad_sum = operands
        grad_pre = (upstream.astype(jnp.float32) * slope_rows).astype(jnp.bfloat16)
        out_features = jnp.dot(grad_pre, proj_out, preferred_element_type=jnp.float32).astype(
            jnp.bfloat16
        )
        grad_sum = grad_sum + lax.dot_general(
            feature_rows, out_features, (((0,), (0,)), ((), ())), preferred_element_type=jnp.float32
        )
        own_grads = lax.dot_general(
            grad_pre, weight_rows, (((1,), (1,)), ((), ())), preferred_element_type=jnp.float32
        ).astype(jnp.bfloat16)
        return (own_grads, grad_sum)

    def block_skip(operands):
        return (jnp.zeros((MICRO, slice_width), jnp.bfloat16), operands[3])

    def prepare(turn_index, upstream_in):
        block_index = turn_index.astype(jnp.int32) - chain_depth
        active = jnp.logical_and(block_index >= 0, block_index < blocks)
        row_start = jnp.clip(block_index, 0, blocks - 1) * MICRO
        top_rows = take_rows(out_grad, row_start)
        upstream = jnp.where(at_top, top_rows, upstream_in)
        return (active, row_start, upstream)

    def turn(turn_index, loop_state):
        incoming, grad_sum = loop_state
        active, row_start, upstream = prepare(turn_index, incoming)
        own_grads, grad_sum = lax.cond(
            active,
            block_grad,
            block_skip,
            (upstream, take_rows(slopes, row_start), take_rows(in_features, row_start), grad_sum),
        )
        full_grads = lax.all_gather(own_grads, "tensor", axis=1, tiled=True)

        def finish(operands):
            upstream_rows, grad_rows, normed_rows, radius_rows = operands
            scaled = grad_rows.astype(jnp.float32) * gain_row
            mean_dot = jnp.mean(scaled * normed_rows, axis=1, keepdims=True)
            return (
                upstream_rows.astype(jnp.float32) + (scaled - normed_rows * mean_dot) / radius_rows
            ).astype(jnp.bfloat16)

        def vacant(operands):
            return jnp.zeros((MICRO, feature_width), jnp.bfloat16)

        outgoing = lax.cond(
            active,
            finish,
            vacant,
            (upstream, full_grads, take_rows(normed, row_start), take_rows(radius, row_start)),
        )
        received = passed_along(outgoing, "section", -1)
        return (received, grad_sum)

    start_state = (jnp.zeros((MICRO, feature_width), jnp.bfloat16), jnp.zeros((R, R), jnp.float32))
    received, grad_sum = lax.fori_loop(0, turn_count, turn, start_state)
    flattened = grad_sum.reshape(R * R)
    piece_width = R * R // split_count
    own_part = lax.dynamic_slice_in_dim(flattened, split_index * piece_width, piece_width, 0)
    seq_index = data_index // (data_count // SEQS)
    seq_mask = (lax.broadcasted_iota(jnp.int32, (SEQS, 1), 0) == seq_index).astype(jnp.float32)
    per_seq = seq_mask * own_part[None, :]
    grads_all = lax.psum(per_seq, "dp")
    queries = query_grads[0].astype(jnp.float32)
    partial_scores = jnp.dot(grads_all, queries.T, precision=lax.Precision.HIGHEST)
    scores = lax.psum(partial_scores, ("section", "tensor"))
    return (grads_all[None], scores)


def solution(mesh):
    in_specs = (
        P("section", "dp", None),
        P("section", "tensor", "dp"),
        P("section", None),
        P("section", None),
        P("dp", None),
        P("section", "dp", "tensor"),
    )
    out_specs = (P("section", None, "tensor"), P(None, "dp"))
    return jax.shard_map(body, mesh=mesh, in_specs=in_specs, out_specs=out_specs, check_vma=False)
```

profile of v0, /device:TPU:1, one launch (start us, length us, event | category | flops | bytes accessed | tf_op | source)
XLA Modules:
  0.0 457.9 jit_solution(3057841927889815034)
XLA Ops:
  11.0 88.2 %all-gather.3.cloned.1.call-done = bf16[1,1024,4096]{2,1,0:T(8,128)(2,1)} async-done(((bf16[1,1024,1024]{2,1,0:T(8,128)(2,1)}), bf16[1,1024,4096]{2,1,0:T(8,128)(2,1)}) %all-gather.3.cloned.1.call-update) | async-done | bytes 8388624 | tf_op jit(solution)/shard_map/all_gather | solution.py:52
  99.3 5.7 %convolution_convert_fusion.2 = bf16[128,4096]{1,0:T(8,128)(2,1)} fusion(bf16[128,4096]{1,0:T(8,128)(2,1)S(1)} %get-tuple-element.421, s32[]{:T(128)S(6)} %select_n.44, bf16[1,1024,4096]{2,1,0:T(8,128)(2,1)} %all-gather.3.cloned.1.call-done), kind=kOutput, calls=%fused_computation.21 | convolution fusion | flops 1074266112 | bytes 9699332 | tf_op jit(solution)/shard_map/dot_general | solution.py:54
  111.4 45.8 %all-reduce.2.cloned.1.call-done = bf16[128,4096]{1,0:T(8,128)(2,1)} async-done(((bf16[128,4096]{1,0:T(8,128)(2,1)}), bf16[128,4096]{1,0:T(8,128)(2,1)}) %all-reduce.2.cloned.1.call-update) | async-done | bytes 1048592 | tf_op jit(solution)/shard_map/psum | solution.py:55
  159.8 263.6 %while.19 = (s32[]{:T(128)}, bf16[16,4096]{1,0:T(8,128)(2,1)S(1)}, f32[64,64]{1,0:T(8,128)}, s32[]{:T(128)}, pred[]{:T(512)}, /*index=5*/bf16[128,4096]{1,0:T(8,...) while((s32[]{:T(128)}, bf16[16,4096]{1,0:T(8,128)(2,1)S(1)}, ...), condition=%wide.region_8.9_spmd.clone, body=%wide.region_2.8_spmd.clone.sunk | while | flops 147674128 | bytes 13017286 | solution.py:121
  159.9 2.3 multiply_convert_fusion.9
  163.2 7.4 %conditional.6 = (bf16[16,1024]{1,0:T(8,128)(2,1)S(1)}, f32[64,64]{1,0:T(8,128)}) conditional(s32[]{:T(128)} %convert_element_type.134, f32[64,64]{1,0:T(8,128)} %get-tuple-element.548, (bf16[16,4096]{1,0:T(8,128)(2,1)S(1)}, f32[128,4096]{1,0:T(8,128)S(1)}, s32[]{:T(128)}, bf16[1024,4096]{1,0:T(8,128)(2,1)}, bf16[128,64]{1,0:T(8,128)(2,1)}, ...), branch_computations={%region_3.3_spmd, %region_4.4_spmd} | conditional | flops 143152128 | bytes 10310676 | solution.py:92
  163.2 5.6 %convolution_convert_fusion = bf16[16,1024]{1,0:T(8,128)(2,1)S(1)} fusion(bf16[1024,4096]{1,0:T(8,128)(2,1)} %get-tuple-element.308, f32[128,4096]{1,0:T(8,128)S(1)} %get-tuple-element.306, s32[]{:T(128)} %get-tuple-element.307, bf16[16,4096]{1,0:T(8,128)(2,1)S(1)} %get-tuple-element.305), kind=kOutput, calls=%fused_computation.1 | convolution fusion | flops 134430720 | bytes 8814596 | tf_op jit(solution)/shard_map/while/body/eval_jaxpr/cond/branch_1_fun/dot_general | solution.py:73
  170.6 10.4 %all_gather.13 = bf16[16,4096]{1,0:T(8,128)(2,1)S(1)} all-gather(bf16[16,1024]{1,0:T(8,128)(2,1)S(1)} %get-tuple-element.519), channel_id=1, replica_groups=mesh['section'=2,'dp'=4,'tensor'=4] {'tensor'}, dimensions={1}, use_global_device_ids=true | all-gather | bytes 163840 | tf_op jit(solution)/shard_map/while/body/eval_jaxpr/all_gather | solution.py:98
  181.1 2.4 conditional.7
  189.0 7.4 %conditional.6 = (bf16[16,1024]{1,0:T(8,128)(2,1)S(1)}, f32[64,64]{1,0:T(8,128)}) conditional(s32[]{:T(128)} %convert_element_type.134, f32[64,64]{1,0:T(8,128)} %get-tuple-element.548, (bf16[16,4096]{1,0:T(8,128)(2,1)S(1)}, f32[128,4096]{1,0:T(8,128)S(1)}, s32[]{:T(128)}, bf16[1024,4096]{1,0:T(8,128)(2,1)}, bf16[128,64]{1,0:T(8,128)(2,1)}, ...), branch_computations={%region_3.3_spmd, %region_4.4_spmd} | conditional | flops 143152128 | bytes 10310676 | solution.py:92
  189.0 5.6 %convolution_convert_fusion = bf16[16,1024]{1,0:T(8,128)(2,1)S(1)} fusion(bf16[1024,4096]{1,0:T(8,128)(2,1)} %get-tuple-element.308, f32[128,4096]{1,0:T(8,128)S(1)} %get-tuple-element.306, s32[]{:T(128)} %get-tuple-element.307, bf16[16,4096]{1,0:T(8,128)(2,1)S(1)} %get-tuple-element.305), kind=kOutput, calls=%fused_computation.1 | convolution fusion | flops 134430720 | bytes 8814596 | tf_op jit(solution)/shard_map/while/body/eval_jaxpr/cond/branch_1_fun/dot_general | solution.py:73
  196.4 10.5 %all_gather.13 = bf16[16,4096]{1,0:T(8,128)(2,1)S(1)} all-gather(bf16[16,1024]{1,0:T(8,128)(2,1)S(1)} %get-tuple-element.519), channel_id=1, replica_groups=mesh['section'=2,'dp'=4,'tensor'=4] {'tensor'}, dimensions={1}, use_global_device_ids=true | all-gather | bytes 163840 | tf_op jit(solution)/shard_map/while/body/eval_jaxpr/all_gather | solution.py:98
  206.9 2.4 conditional.7
  209.3 5.2 %collective-permute-start = (bf16[16,4096]{1,0:T(8,128)(2,1)S(1)}, bf16[16,4096]{1,0:T(8,128)(2,1)S(1)}, u32[]{:S(2)}, u32[]{:S(2)}) collective-permute-start(bf16[16,4096]{1,0:T(8,128)(2,1)S(1)} %get-tuple-element.588), channel_id=1, source_target_pairs={{16,0},{17,1},{18,2},{19,3},{20,4},{21,5},{22,6},{23,7},{24,8},{25... | collective-permute-start | bytes 393224 | tf_op jit(solution)/shard_map/while/body/eval_jaxpr/ppermute | solution.py:16
  215.5 2.3 multiply_convert_fusion.9
  218.8 7.4 %conditional.6 = (bf16[16,1024]{1,0:T(8,128)(2,1)S(1)}, f32[64,64]{1,0:T(8,128)}) conditional(s32[]{:T(128)} %convert_element_type.134, f32[64,64]{1,0:T(8,128)} %get-tuple-element.548, (bf16[16,4096]{1,0:T(8,128)(2,1)S(1)}, f32[128,4096]{1,0:T(8,128)S(1)}, s32[]{:T(128)}, bf16[1024,4096]{1,0:T(8,128)(2,1)}, bf16[128,64]{1,0:T(8,128)(2,1)}, ...), branch_computations={%region_3.3_spmd, %region_4.4_spmd} | conditional | flops 143152128 | bytes 10310676 | solution.py:92
  218.8 5.6 %convolution_convert_fusion = bf16[16,1024]{1,0:T(8,128)(2,1)S(1)} fusion(bf16[1024,4096]{1,0:T(8,128)(2,1)} %get-tuple-element.308, f32[128,4096]{1,0:T(8,128)S(1)} %get-tuple-element.306, s32[]{:T(128)} %get-tuple-element.307, bf16[16,4096]{1,0:T(8,128)(2,1)S(1)} %get-tuple-element.305), kind=kOutput, calls=%fused_computation.1 | convolution fusion | flops 134430720 | bytes 8814596 | tf_op jit(solution)/shard_map/while/body/eval_jaxpr/cond/branch_1_fun/dot_general | solution.py:73
  226.2 10.5 %all_gather.13 = bf16[16,4096]{1,0:T(8,128)(2,1)S(1)} all-gather(bf16[16,1024]{1,0:T(8,128)(2,1)S(1)} %get-tuple-element.519), channel_id=1, replica_groups=mesh['section'=2,'dp'=4,'tensor'=4] {'tensor'}, dimensions={1}, use_global_device_ids=true | all-gather | bytes 163840 | tf_op jit(solution)/shard_map/while/body/eval_jaxpr/all_gather | solution.py:98
  236.7 2.4 conditional.7
  239.1 5.2 %collective-permute-start = (bf16[16,4096]{1,0:T(8,128)(2,1)S(1)}, bf16[16,4096]{1,0:T(8,128)(2,1)S(1)}, u32[]{:S(2)}, u32[]{:S(2)}) collective-permute-start(bf16[16,4096]{1,0:T(8,128)(2,1)S(1)} %get-tuple-element.588), channel_id=1, source_target_pairs={{16,0},{17,1},{18,2},{19,3},{20,4},{21,5},{22,6},{23,7},{24,8},{25... | collective-permute-start | bytes 393224 | tf_op jit(solution)/shard_map/while/body/eval_jaxpr/ppermute | solution.py:16
  248.5 7.4 %conditional.6 = (bf16[16,1024]{1,0:T(8,128)(2,1)S(1)}, f32[64,64]{1,0:T(8,128)}) conditional(s32[]{:T(128)} %convert_element_type.134, f32[64,64]{1,0:T(8,128)} %get-tuple-element.548, (bf16[16,4096]{1,0:T(8,128)(2,1)S(1)}, f32[128,4096]{1,0:T(8,128)S(1)}, s32[]{:T(128)}, bf16[1024,4096]{1,0:T(8,128)(2,1)}, bf16[128,64]{1,0:T(8,128)(2,1)}, ...), branch_computations={%region_3.3_spmd, %region_4.4_spmd} | conditional | flops 143152128 | bytes 10310676 | solution.py:92
  248.5 5.6 %convolution_convert_fusion = bf16[16,1024]{1,0:T(8,128)(2,1)S(1)} fusion(bf16[1024,4096]{1,0:T(8,128)(2,1)} %get-tuple-element.308, f32[128,4096]{1,0:T(8,128)S(1)} %get-tuple-element.306, s32[]{:T(128)} %get-tuple-element.307, bf16[16,4096]{1,0:T(8,128)(2,1)S(1)} %get-tuple-element.305), kind=kOutput, calls=%fused_computation.1 | convolution fusion | flops 134430720 | bytes 8814596 | tf_op jit(solution)/shard_map/while/body/eval_jaxpr/cond/branch_1_fun/dot_general | solution.py:73
  256.0 10.5 %all_gather.13 = bf16[16,4096]{1,0:T(8,128)(2,1)S(1)} all-gather(bf16[16,1024]{1,0:T(8,128)(2,1)S(1)} %get-tuple-element.519), channel_id=1, replica_groups=mesh['section'=2,'dp'=4,'tensor'=4] {'tensor'}, dimensions={1}, use_global_device_ids=true | all-gather | bytes 163840 | tf_op jit(solution)/shard_map/while/body/eval_jaxpr/all_gather | solution.py:98
  266.4 2.4 conditional.7
  268.8 5.2 %collective-permute-start = (bf16[16,4096]{1,0:T(8,128)(2,1)S(1)}, bf16[16,4096]{1,0:T(8,128)(2,1)S(1)}, u32[]{:S(2)}, u32[]{:S(2)}) collective-permute-start(bf16[16,4096]{1,0:T(8,128)(2,1)S(1)} %get-tuple-element.588), channel_id=1, source_target_pairs={{16,0},{17,1},{18,2},{19,3},{20,4},{21,5},{22,6},{23,7},{24,8},{25... | collective-permute-start | bytes 393224 | tf_op jit(solution)/shard_map/while/body/eval_jaxpr/ppermute | solution.py:16
  278.2 7.4 %conditional.6 = (bf16[16,1024]{1,0:T(8,128)(2,1)S(1)}, f32[64,64]{1,0:T(8,128)}) conditional(s32[]{:T(128)} %convert_element_type.134, f32[64,64]{1,0:T(8,128)} %get-tuple-element.548, (bf16[16,4096]{1,0:T(8,128)(2,1)S(1)}, f32[128,4096]{1,0:T(8,128)S(1)}, s32[]{:T(128)}, bf16[1024,4096]{1,0:T(8,128)(2,1)}, bf16[128,64]{1,0:T(8,128)(2,1)}, ...), branch_computations={%region_3.3_spmd, %region_4.4_spmd} | conditional | flops 143152128 | bytes 10310676 | solution.py:92
  278.3 5.6 %convolution_convert_fusion = bf16[16,1024]{1,0:T(8,128)(2,1)S(1)} fusion(bf16[1024,4096]{1,0:T(8,128)(2,1)} %get-tuple-element.308, f32[128,4096]{1,0:T(8,128)S(1)} %get-tuple-element.306, s32[]{:T(128)} %get-tuple-element.307, bf16[16,4096]{1,0:T(8,128)(2,1)S(1)} %get-tuple-element.305), kind=kOutput, calls=%fused_computation.1 | convolution fusion | flops 134430720 | bytes 8814596 | tf_op jit(solution)/shard_map/while/body/eval_jaxpr/cond/branch_1_fun/dot_general | solution.py:73
  285.7 10.5 %all_gather.13 = bf16[16,4096]{1,0:T(8,128)(2,1)S(1)} all-gather(bf16[16,1024]{1,0:T(8,128)(2,1)S(1)} %get-tuple-element.519), channel_id=1, replica_groups=mesh['section'=2,'dp'=4,'tensor'=4] {'tensor'}, dimensions={1}, use_global_device_ids=true | all-gather | bytes 163840 | tf_op jit(solution)/shard_map/while/body/eval_jaxpr/all_gather | solution.py:98
  296.2 2.4 conditional.7
  298.5 5.2 %collective-permute-start = (bf16[16,4096]{1,0:T(8,128)(2,1)S(1)}, bf16[16,4096]{1,0:T(8,128)(2,1)S(1)}, u32[]{:S(2)}, u32[]{:S(2)}) collective-permute-start(bf16[16,4096]{1,0:T(8,128)(2,1)S(1)} %get-tuple-element.588), channel_id=1, source_target_pairs={{16,0},{17,1},{18,2},{19,3},{20,4},{21,5},{22,6},{23,7},{24,8},{25... | collective-permute-start | bytes 393224 | tf_op jit(solution)/shard_map/while/body/eval_jaxpr/ppermute | solution.py:16
  308.0 7.4 %conditional.6 = (bf16[16,1024]{1,0:T(8,128)(2,1)S(1)}, f32[64,64]{1,0:T(8,128)}) conditional(s32[]{:T(128)} %convert_element_type.134, f32[64,64]{1,0:T(8,128)} %get-tuple-element.548, (bf16[16,4096]{1,0:T(8,128)(2,1)S(1)}, f32[128,4096]{1,0:T(8,128)S(1)}, s32[]{:T(128)}, bf16[1024,4096]{1,0:T(8,128)(2,1)}, bf16[128,64]{1,0:T(8,128)(2,1)}, ...), branch_computations={%region_3.3_spmd, %region_4.4_spmd} | conditional | flops 143152128 | bytes 10310676 | solution.py:92
  308.0 5.6 %convolution_convert_fusion = bf16[16,1024]{1,0:T(8,128)(2,1)S(1)} fusion(bf16[1024,4096]{1,0:T(8,128)(2,1)} %get-tuple-element.308, f32[128,4096]{1,0:T(8,128)S(1)} %get-tuple-element.306, s32[]{:T(128)} %get-tuple-element.307, bf16[16,4096]{1,0:T(8,128)(2,1)S(1)} %get-tuple-element.305), kind=kOutput, calls=%fused_computation.1 | convolution fusion | flops 134430720 | bytes 8814596 | tf_op jit(solution)/shard_map/while/body/eval_jaxpr/cond/branch_1_fun/dot_general | solution.py:73
  315.4 10.5 %all_gather.13 = bf16[16,4096]{1,0:T(8,128)(2,1)S(1)} all-gather(bf16[16,1024]{1,0:T(8,128)(2,1)S(1)} %get-tuple-element.519), channel_id=1, replica_groups=mesh['section'=2,'dp'=4,'tensor'=4] {'tensor'}, dimensions={1}, use_global_device_ids=true | all-gather | bytes 163840 | tf_op jit(solution)/shard_map/while/body/eval_jaxpr/all_gather | solution.py:98
  325.9 2.4 conditional.7
  328.3 5.2 %collective-permute-start = (bf16[16,4096]{1,0:T(8,128)(2,1)S(1)}, bf16[16,4096]{1,0:T(8,128)(2,1)S(1)}, u32[]{:S(2)}, u32[]{:S(2)}) collective-permute-start(bf16[16,4096]{1,0:T(8,128)(2,1)S(1)} %get-tuple-element.588), channel_id=1, source_target_pairs={{16,0},{17,1},{18,2},{19,3},{20,4},{21,5},{22,6},{23,7},{24,8},{25... | collective-permute-start | bytes 393224 | tf_op jit(solution)/shard_map/while/body/eval_jaxpr/ppermute | solution.py:16
  337.7 7.4 %conditional.6 = (bf16[16,1024]{1,0:T(8,128)(2,1)S(1)}, f32[64,64]{1,0:T(8,128)}) conditional(s32[]{:T(128)} %convert_element_type.134, f32[64,64]{1,0:T(8,128)} %get-tuple-element.548, (bf16[16,4096]{1,0:T(8,128)(2,1)S(1)}, f32[128,4096]{1,0:T(8,128)S(1)}, s32[]{:T(128)}, bf16[1024,4096]{1,0:T(8,128)(2,1)}, bf16[128,64]{1,0:T(8,128)(2,1)}, ...), branch_computations={%region_3.3_spmd, %region_4.4_spmd} | conditional | flops 143152128 | bytes 10310676 | solution.py:92
  337.7 5.6 %convolution_convert_fusion = bf16[16,1024]{1,0:T(8,128)(2,1)S(1)} fusion(bf16[1024,4096]{1,0:T(8,128)(2,1)} %get-tuple-element.308, f32[128,4096]{1,0:T(8,128)S(1)} %get-tuple-element.306, s32[]{:T(128)} %get-tuple-element.307, bf16[16,4096]{1,0:T(8,128)(2,1)S(1)} %get-tuple-element.305), kind=kOutput, calls=%fused_computation.1 | convolution fusion | flops 134430720 | bytes 8814596 | tf_op jit(solution)/shard_map/while/body/eval_jaxpr/cond/branch_1_fun/dot_general | solution.py:73
  345.1 10.5 %all_gather.13 = bf16[16,4096]{1,0:T(8,128)(2,1)S(1)} all-gather(bf16[16,1024]{1,0:T(8,128)(2,1)S(1)} %get-tuple-element.519), channel_id=1, replica_groups=mesh['section'=2,'dp'=4,'tensor'=4] {'tensor'}, dimensions={1}, use_global_device_ids=true | all-gather | bytes 163840 | tf_op jit(solution)/shard_map/while/body/eval_jaxpr/all_gather | solution.py:98
  355.6 2.4 conditional.7
  358.0 5.2 %collective-permute-start = (bf16[16,4096]{1,0:T(8,128)(2,1)S(1)}, bf16[16,4096]{1,0:T(8,128)(2,1)S(1)}, u32[]{:S(2)}, u32[]{:S(2)}) collective-permute-start(bf16[16,4096]{1,0:T(8,128)(2,1)S(1)} %get-tuple-element.588), channel_id=1, source_target_pairs={{16,0},{17,1},{18,2},{19,3},{20,4},{21,5},{22,6},{23,7},{24,8},{25... | collective-permute-start | bytes 393224 | tf_op jit(solution)/shard_map/while/body/eval_jaxpr/ppermute | solution.py:16
  367.4 7.4 %conditional.6 = (bf16[16,1024]{1,0:T(8,128)(2,1)S(1)}, f32[64,64]{1,0:T(8,128)}) conditional(s32[]{:T(128)} %convert_element_type.134, f32[64,64]{1,0:T(8,128)} %get-tuple-element.548, (bf16[16,4096]{1,0:T(8,128)(2,1)S(1)}, f32[128,4096]{1,0:T(8,128)S(1)}, s32[]{:T(128)}, bf16[1024,4096]{1,0:T(8,128)(2,1)}, bf16[128,64]{1,0:T(8,128)(2,1)}, ...), branch_computations={%region_3.3_spmd, %region_4.4_spmd} | conditional | flops 143152128 | bytes 10310676 | solution.py:92
  367.4 5.6 %convolution_convert_fusion = bf16[16,1024]{1,0:T(8,128)(2,1)S(1)} fusion(bf16[1024,4096]{1,0:T(8,128)(2,1)} %get-tuple-element.308, f32[128,4096]{1,0:T(8,128)S(1)} %get-tuple-element.306, s32[]{:T(128)} %get-tuple-element.307, bf16[16,4096]{1,0:T(8,128)(2,1)S(1)} %get-tuple-element.305), kind=kOutput, calls=%fused_computation.1 | convolution fusion | flops 134430720 | bytes 8814596 | tf_op jit(solution)/shard_map/while/body/eval_jaxpr/cond/branch_1_fun/dot_general | solution.py:73
  374.9 10.5 %all_gather.13 = bf16[16,4096]{1,0:T(8,128)(2,1)S(1)} all-gather(bf16[16,1024]{1,0:T(8,128)(2,1)S(1)} %get-tuple-element.519), channel_id=1, replica_groups=mesh['section'=2,'dp'=4,'tensor'=4] {'tensor'}, dimensions={1}, use_global_device_ids=true | all-gather | bytes 163840 | tf_op jit(solution)/shard_map/while/body/eval_jaxpr/all_gather | solution.py:98
  387.6 5.3 %collective-permute-start = (bf16[16,4096]{1,0:T(8,128)(2,1)S(1)}, bf16[16,4096]{1,0:T(8,128)(2,1)S(1)}, u32[]{:S(2)}, u32[]{:S(2)}) collective-permute-start(bf16[16,4096]{1,0:T(8,128)(2,1)S(1)} %get-tuple-element.588), channel_id=1, source_target_pairs={{16,0},{17,1},{18,2},{19,3},{20,4},{21,5},{22,6},{23,7},{24,8},{25... | collective-permute-start | bytes 393224 | tf_op jit(solution)/shard_map/while/body/eval_jaxpr/ppermute | solution.py:16
  397.2 10.5 %all_gather.13 = bf16[16,4096]{1,0:T(8,128)(2,1)S(1)} all-gather(bf16[16,1024]{1,0:T(8,128)(2,1)S(1)} %get-tuple-element.519), channel_id=1, replica_groups=mesh['section'=2,'dp'=4,'tensor'=4] {'tensor'}, dimensions={1}, use_global_device_ids=true | all-gather | bytes 163840 | tf_op jit(solution)/shard_map/while/body/eval_jaxpr/all_gather | solution.py:98
  407.7 14.8 %collective-permute-start = (bf16[16,4096]{1,0:T(8,128)(2,1)S(1)}, bf16[16,4096]{1,0:T(8,128)(2,1)S(1)}, u32[]{:S(2)}, u32[]{:S(2)}) collective-permute-start(bf16[16,4096]{1,0:T(8,128)(2,1)S(1)} %get-tuple-element.588), channel_id=1, source_target_pairs={{16,0},{17,1},{18,2},{19,3},{20,4},{21,5},{22,6},{23,7},{24,8},{25... | collective-permute-start | bytes 393224 | tf_op jit(solution)/shard_map/while/body/eval_jaxpr/ppermute | solution.py:16
  425.0 7.8 %psum.22 = f32[2,1024]{1,0:T(2,128)S(1)} all-reduce(f32[2,1024]{1,0:T(2,128)S(1)} %broadcast_multiply_fusion.1), channel_id=1, replica_groups=mesh['section'=2,'dp'=4,'tensor'=4] {'dp'}, use_global_device_ids=true, to_apply=%region_9.10 | all-reduce | flops 2048 | bytes 16384 | tf_op jit(solution)/shard_map/psum | solution.py:128
  433.0 18.1 %psum.23 = f32[2,64]{1,0:T(2,128)} all-reduce(f32[2,64]{1,0:T(2,128)S(1)} %fusion.32), channel_id=1, replica_groups=mesh['section'=2,'dp'=4,'tensor'=4] {'section','tensor'}, use_global_device_ids=true, to_apply=%region_10.11 | all-reduce | flops 128 | bytes 1024 | tf_op jit(solution)/shard_map/psum | solution.py:131
  (119 shorter events, 83.3 us)
Async XLA Ops:
  7.2 425.6 %copy-start = (bf16[1,64,1024]{2,1,0:T(8,128)(2,1)S(1)}, bf16[1,64,1024]{2,1,0:T(8,128)(2,1)}, u32[]{:S(2)}) copy-start(bf16[1,64,1024]{2,1,0:T(8,128)(2,1)} %param.17) | copy-start | bytes 393220
  7.2 1.3 copy-start.1
  7.2 2.1 copy-start.2
  7.2 92.1 %all-gather.3.cloned.1.call-start = ((), (), s32[]{:S(2)}) async-start(), calls=%async_computation.1 | async-start | bytes 10485760 | tf_op jit(solution)/shard_map/all_gather | solution.py:52
  7.9 149.3 %all-reduce.2.cloned.1.call-start = ((), (), s32[]{:S(2)}) async-start(), calls=%async_computation | async-start | bytes 2097152 | tf_op jit(solution)/shard_map/psum | solution.py:55
  99.3 5.7 %copy-start.4 = (s32[1,2]{1,0:T(1,128)S(1)}, s32[1,2]{1,0:T(1,128)}, u32[]{:S(2)}) copy-start(s32[1,2]{1,0:T(1,128)} %param.15) | copy-start | bytes 28
  163.2 17.9 %copy-start.5 = (f32[128,1]{0,1:T(1,128)S(1)}, f32[128,1]{0,1:T(1,128)}, u32[]{:S(2)}) copy-start(f32[128,1]{0,1:T(1,128)} %get-tuple-element.578) | copy-start | bytes 1540 | tf_op jit(solution)/shard_map/while
  183.4 2.3 collective-permute-start
  189.0 17.9 %copy-start.5 = (f32[128,1]{0,1:T(1,128)S(1)}, f32[128,1]{0,1:T(1,128)}, u32[]{:S(2)}) copy-start(f32[128,1]{0,1:T(1,128)} %get-tuple-element.578) | copy-start | bytes 1540 | tf_op jit(solution)/shard_map/while
  209.3 6.2 %collective-permute-start = (bf16[16,4096]{1,0:T(8,128)(2,1)S(1)}, bf16[16,4096]{1,0:T(8,128)(2,1)S(1)}, u32[]{:S(2)}, u32[]{:S(2)}) collective-permute-start(bf16[16,4096]{1,0:T(8,128)(2,1)S(1)} %get-tuple-element.588), channel_id=1, source_target_pairs={{16,0},{17,1},{18,2},{19,3},{20,4},{21,5},{22,6},{23,7},{24,8},{25... | collective-permute-start | bytes 393224 | tf_op jit(solution)/shard_map/while/body/eval_jaxpr/ppermute | solution.py:16
  218.8 17.9 %copy-start.5 = (f32[128,1]{0,1:T(1,128)S(1)}, f32[128,1]{0,1:T(1,128)}, u32[]{:S(2)}) copy-start(f32[128,1]{0,1:T(1,128)} %get-tuple-element.578) | copy-start | bytes 1540 | tf_op jit(solution)/shard_map/while
  239.1 6.2 %collective-permute-start = (bf16[16,4096]{1,0:T(8,128)(2,1)S(1)}, bf16[16,4096]{1,0:T(8,128)(2,1)S(1)}, u32[]{:S(2)}, u32[]{:S(2)}) collective-permute-start(bf16[16,4096]{1,0:T(8,128)(2,1)S(1)} %get-tuple-element.588), channel_id=1, source_target_pairs={{16,0},{17,1},{18,2},{19,3},{20,4},{21,5},{22,6},{23,7},{24,8},{25... | collective-permute-start | bytes 393224 | tf_op jit(solution)/shard_map/while/body/eval_jaxpr/ppermute | solution.py:16
  248.5 17.9 %copy-start.5 = (f32[128,1]{0,1:T(1,128)S(1)}, f32[128,1]{0,1:T(1,128)}, u32[]{:S(2)}) copy-start(f32[128,1]{0,1:T(1,128)} %get-tuple-element.578) | copy-start | bytes 1540 | tf_op jit(solution)/shard_map/while
  268.8 6.1 %collective-permute-start = (bf16[16,4096]{1,0:T(8,128)(2,1)S(1)}, bf16[16,4096]{1,0:T(8,128)(2,1)S(1)}, u32[]{:S(2)}, u32[]{:S(2)}) collective-permute-start(bf16[16,4096]{1,0:T(8,128)(2,1)S(1)} %get-tuple-element.588), channel_id=1, source_target_pairs={{16,0},{17,1},{18,2},{19,3},{20,4},{21,5},{22,6},{23,7},{24,8},{25... | collective-permute-start | bytes 393224 | tf_op jit(solution)/shard_map/while/body/eval_jaxpr/ppermute | solution.py:16
  278.2 17.9 %copy-start.5 = (f32[128,1]{0,1:T(1,128)S(1)}, f32[128,1]{0,1:T(1,128)}, u32[]{:S(2)}) copy-start(f32[128,1]{0,1:T(1,128)} %get-tuple-element.578) | copy-start | bytes 1540 | tf_op jit(solution)/shard_map/while
  298.5 6.1 %collective-permute-start = (bf16[16,4096]{1,0:T(8,128)(2,1)S(1)}, bf16[16,4096]{1,0:T(8,128)(2,1)S(1)}, u32[]{:S(2)}, u32[]{:S(2)}) collective-permute-start(bf16[16,4096]{1,0:T(8,128)(2,1)S(1)} %get-tuple-element.588), channel_id=1, source_target_pairs={{16,0},{17,1},{18,2},{19,3},{20,4},{21,5},{22,6},{23,7},{24,8},{25... | collective-permute-start | bytes 393224 | tf_op jit(solution)/shard_map/while/body/eval_jaxpr/ppermute | solution.py:16
  308.0 17.9 %copy-start.5 = (f32[128,1]{0,1:T(1,128)S(1)}, f32[128,1]{0,1:T(1,128)}, u32[]{:S(2)}) copy-start(f32[128,1]{0,1:T(1,128)} %get-tuple-element.578) | copy-start | bytes 1540 | tf_op jit(solution)/shard_map/while
  328.3 6.1 %collective-permute-start = (bf16[16,4096]{1,0:T(8,128)(2,1)S(1)}, bf16[16,4096]{1,0:T(8,128)(2,1)S(1)}, u32[]{:S(2)}, u32[]{:S(2)}) collective-permute-start(bf16[16,4096]{1,0:T(8,128)(2,1)S(1)} %get-tuple-element.588), channel_id=1, source_target_pairs={{16,0},{17,1},{18,2},{19,3},{20,4},{21,5},{22,6},{23,7},{24,8},{25... | collective-permute-start | bytes 393224 | tf_op jit(solution)/shard_map/while/body/eval_jaxpr/ppermute | solution.py:16
  337.7 17.9 %copy-start.5 = (f32[128,1]{0,1:T(1,128)S(1)}, f32[128,1]{0,1:T(1,128)}, u32[]{:S(2)}) copy-start(f32[128,1]{0,1:T(1,128)} %get-tuple-element.578) | copy-start | bytes 1540 | tf_op jit(solution)/shard_map/while
  358.0 6.1 %collective-permute-start = (bf16[16,4096]{1,0:T(8,128)(2,1)S(1)}, bf16[16,4096]{1,0:T(8,128)(2,1)S(1)}, u32[]{:S(2)}, u32[]{:S(2)}) collective-permute-start(bf16[16,4096]{1,0:T(8,128)(2,1)S(1)} %get-tuple-element.588), channel_id=1, source_target_pairs={{16,0},{17,1},{18,2},{19,3},{20,4},{21,5},{22,6},{23,7},{24,8},{25... | collective-permute-start | bytes 393224 | tf_op jit(solution)/shard_map/while/body/eval_jaxpr/ppermute | solution.py:16
  367.4 17.9 %copy-start.5 = (f32[128,1]{0,1:T(1,128)S(1)}, f32[128,1]{0,1:T(1,128)}, u32[]{:S(2)}) copy-start(f32[128,1]{0,1:T(1,128)} %get-tuple-element.578) | copy-start | bytes 1540 | tf_op jit(solution)/shard_map/while
  387.6 6.2 %collective-permute-start = (bf16[16,4096]{1,0:T(8,128)(2,1)S(1)}, bf16[16,4096]{1,0:T(8,128)(2,1)S(1)}, u32[]{:S(2)}, u32[]{:S(2)}) collective-permute-start(bf16[16,4096]{1,0:T(8,128)(2,1)S(1)} %get-tuple-element.588), channel_id=1, source_target_pairs={{16,0},{17,1},{18,2},{19,3},{20,4},{21,5},{22,6},{23,7},{24,8},{25... | collective-permute-start | bytes 393224 | tf_op jit(solution)/shard_map/while/body/eval_jaxpr/ppermute | solution.py:16
  397.1 10.5 %copy-start.5 = (f32[128,1]{0,1:T(1,128)S(1)}, f32[128,1]{0,1:T(1,128)}, u32[]{:S(2)}) copy-start(f32[128,1]{0,1:T(1,128)} %get-tuple-element.578) | copy-start | bytes 1540 | tf_op jit(solution)/shard_map/while
  407.7 15.8 %collective-permute-start = (bf16[16,4096]{1,0:T(8,128)(2,1)S(1)}, bf16[16,4096]{1,0:T(8,128)(2,1)S(1)}, u32[]{:S(2)}, u32[]{:S(2)}) collective-permute-start(bf16[16,4096]{1,0:T(8,128)(2,1)S(1)} %get-tuple-element.588), channel_id=1, source_target_pairs={{16,0},{17,1},{18,2},{19,3},{20,4},{21,5},{22,6},{23,7},{24,8},{25... | collective-permute-start | bytes 393224 | tf_op jit(solution)/shard_map/while/body/eval_jaxpr/ppermute | solution.py:16
  432.8 18.3 %copy-start.3 = (f32[2,1024]{1,0:T(2,128)}, f32[2,1024]{1,0:T(2,128)S(1)}, u32[]{:S(2)}) copy-start(f32[2,1024]{1,0:T(2,128)S(1)} %psum.22) | copy-start | bytes 24580
Sparse Core Ops, SparseCore 0:
  9.9 89.3 all-gather.2
  105.1 52.1 all-reduce.1
where the time goes:
time: 461 us; the launch traced here: 458 us
  waiting for transfers between devices  143 us (31%)
  blocking collectives  120 us (26%)
  matrix products  67.3 us (15%)
  other arithmetic  54.6 us (12%)
  starting transfers between devices  52.6 us (11%)
  between operations  15.4 us (3%)
    all_gather x9, blocking collectives, turn(): full_grads = lax.all_gather(own_grads, 'tensor', axis=1, tiled=True)  94.2 us
    all_gather x1, waiting for transfers between devices, body(): weight_rows = lax.all_gather(weights[0], 'dp', axis=1, tiled=True)  88.2 us
    ppermute x9, starting transfers between devices, passed_along(): lax.ppermute(value, axis, [(source, source + steps) for source in range(f...  52.5 us
    psum x1, waiting for transfers between devices, body(): lax.psum(partial_value.astype(jnp.bfloat16), 'tensor').astype(jnp.float32)  45.8 us
    dot_general x8, matrix products, block_grad(): lax.dot_general(grad_pre, weight_rows, (((1,), (1,)), ((), ())), preferre...  45.2 us
    convert_element_type x9, other arithmetic, sign_table(): (jnp.where(parity == 1, 1.0, -1.0) * (1.0 / math.sqrt(row_count))).astype...  21 us
    psum x1, blocking collectives, body(): scores = lax.psum(partial_scores, ('section', 'tensor'))  18.1 us
    dot_general x8, matrix products, block_grad(): lax.dot_general(feature_rows, out_features, (((0,), (0,)), ((), ())), pre...  14.2 us
  transfers between devices with their start and end apart: 11, of which 11 were waited for; matrix products, arithmetic and copies ran while one was open for 2% of the time, Pallas kernels for 0%

commit v1 on v0

--- a/solution.py
+++ b/solution.py
@@ -52,7 +52,9 @@
     weight_rows = lax.all_gather(weights[0], "dp", axis=1, tiled=True)
     lifted_own = lax.dynamic_slice_in_dim(lifted, own_start, slice_width, 1)
     partial_value = jnp.dot(lifted_own, weight_rows, preferred_element_type=jnp.float32)
-    summed = lax.psum(partial_value.astype(jnp.bfloat16), "tensor").astype(jnp.float32)
+    summed = jnp.sum(
+        jax.lax.all_gather(partial_value.astype(jnp.bfloat16), "tensor"), axis=0
+    ).astype(jnp.float32)
     sigmoid_z = jax.nn.sigmoid(summed)
     slopes = sigmoid_z * (1.0 + summed * (1.0 - sigmoid_z))
     proj_in = sign_table(proj_seeds[0, 0], feature_width)

time: 461 us -> 504 us (1.093)
  waiting for transfers between devices: 143 us -> 174 us
  local copies, waits for them, and re-layouts: 3.93 us -> 14.1 us
    all_gather x0 -> x1, waiting for transfers between devices: none -> 76.4 us  [body(): jax.lax.all_gather(partial_value.astype(jnp.bfloat16), 'tensor')]
    psum x1 -> x0, waiting for transfers between devices: 45.8 us -> none  [body(): lax.psum(partial_value.astype(jnp.bfloat16), 'tensor').astype(jnp.float32)]
    while x18, local copies, waits for them, and re-layouts: 0.04 us -> 5.39 us
  transfers between devices with their start and end apart: 11 -> 11, of which waited for: 11 -> 11; matrix products, arithmetic and copies ran while one was open for 2% -> 1% of each run, Pallas kernels for 0% -> 0%
where the time goes in v1:
time: 504 us; the launch traced here: 501 us
  waiting for transfers between devices  174 us (35%)
  blocking collectives  121 us (24%)
  matrix products  66.6 us (13%)
  other arithmetic  55.2 us (11%)
  starting transfers between devices  53.6 us (11%)
  between operations  15.4 us (3%)
  local copies, waits for them, and re-layouts  14.1 us (3%)
    all_gather x9, blocking collectives, turn(): full_grads = lax.all_gather(own_grads, 'tensor', axis=1, tiled=True)  96.4 us
    all_gather x1, waiting for transfers between devices, body(): weight_rows = lax.all_gather(weights[0], 'dp', axis=1, tiled=True)  88.3 us
    all_gather x1, waiting for transfers between devices, body(): jax.lax.all_gather(partial_value.astype(jnp.bfloat16), 'tensor')  76.4 us
    ppermute x9, starting transfers between devices, passed_along(): lax.ppermute(value, axis, [(source, source + steps) for source in range(f...  53.5 us
    dot_general x8, matrix products, block_grad(): lax.dot_general(grad_pre, weight_rows, (((1,), (1,)), ((), ())), preferre...  45.2 us
    convert_element_type x9, other arithmetic, sign_table(): (jnp.where(parity == 1, 1.0, -1.0) * (1.0 / math.sqrt(row_count))).astype...  21.1 us
    psum x1, blocking collectives, body(): scores = lax.psum(partial_scores, ('section', 'tensor'))  17 us
    dot_general x8, matrix products, block_grad(): lax.dot_general(feature_rows, out_features, (((0,), (0,)), ((), ())), pre...  14.2 us
  transfers between devices with their start and end apart: 11, of which 11 were waited for; matrix products, arithmetic and copies ran while one was open for 1% of the time, Pallas kernels for 0%

profile of v1, /device:TPU:1, one launch (start us, length us, event | category | flops | bytes accessed | tf_op | source)
XLA Modules:
  0.0 500.9 jit_solution(8214340285332486690)
XLA Ops:
  11.0 88.3 %all-gather.5.cloned.1.call-done = bf16[1,1024,4096]{2,1,0:T(8,128)(2,1)} async-done(((bf16[1,1024,1024]{2,1,0:T(8,128)(2,1)}), bf16[1,1024,4096]{2,1,0:T(8,128)(2,1)}) %all-gather.5.cloned.1.call-update) | async-done | bytes 8388624 | tf_op jit(solution)/shard_map/all_gather | solution.py:52
  99.3 5.6 %convolution_convert_fusion.2 = bf16[128,4096]{1,0:T(8,128)(2,1)} fusion(bf16[128,4096]{1,0:T(8,128)(2,1)S(1)} %get-tuple-element.421, s32[]{:T(128)S(6)} %select_n.44, bf16[1,1024,4096]{2,1,0:T(8,128)(2,1)} %all-gather.5.cloned.1.call-done), kind=kOutput, calls=%fused_computation.21 | convolution fusion | flops 1074266112 | bytes 9699332 | tf_op jit(solution)/shard_map/dot_general | solution.py:54
  109.5 76.4 %all-gather.7.cloned.1.call-done = bf16[512,4096]{1,0:T(8,128)(2,1)} async-done(((bf16[128,4096]{1,0:T(8,128)(2,1)}), bf16[512,4096]{1,0:T(8,128)(2,1)}) %all-gather.7.cloned.1.call-update) | async-done | bytes 4194320 | tf_op jit(solution)/shard_map/all_gather | solution.py:56
  185.9 3.1 reduce_sum.33
  190.3 277.1 %while.19 = (s32[]{:T(128)}, bf16[16,4096]{1,0:T(8,128)(2,1)S(1)}, f32[64,64]{1,0:T(8,128)}, s32[]{:T(128)}, pred[]{:T(512)}, /*index=5*/bf16[128,4096]{1,0:T(8,...) while((s32[]{:T(128)}, bf16[16,4096]{1,0:T(8,128)(2,1)S(1)}, ...), condition=%wide.region_8.9_spmd.clone, body=%wide.region_2.8_spmd.clone.sunk | while | flops 147674128 | bytes 13146310 | solution.py:123
  193.6 7.4 %conditional.6 = (bf16[16,1024]{1,0:T(8,128)(2,1)S(1)}, f32[64,64]{1,0:T(8,128)}) conditional(s32[]{:T(128)} %convert_element_type.136, f32[64,64]{1,0:T(8,128)} %get-tuple-element.548, (bf16[16,4096]{1,0:T(8,128)(2,1)S(1)}, f32[128,4096]{1,0:T(8,128)S(1)}, s32[]{:T(128)}, bf16[1024,4096]{1,0:T(8,128)(2,1)}, bf16[128,64]{1,0:T(8,128)(2,1)}, ...), branch_computations={%region_3.3_spmd, %region_4.4_spmd} | conditional | flops 143152128 | bytes 10310676 | solution.py:94
  193.6 5.6 %convolution_convert_fusion = bf16[16,1024]{1,0:T(8,128)(2,1)S(1)} fusion(bf16[1024,4096]{1,0:T(8,128)(2,1)} %get-tuple-element.308, f32[128,4096]{1,0:T(8,128)S(1)} %get-tuple-element.306, s32[]{:T(128)} %get-tuple-element.307, bf16[16,4096]{1,0:T(8,128)(2,1)S(1)} %get-tuple-element.305), kind=kOutput, calls=%fused_computation.1 | convolution fusion | flops 134430720 | bytes 8814596 | tf_op jit(solution)/shard_map/while/body/eval_jaxpr/cond/branch_1_fun/dot_general | solution.py:75
  201.7 10.7 %all_gather.21 = bf16[16,4096]{1,0:T(8,128)(2,1)S(1)} all-gather(bf16[16,1024]{1,0:T(8,128)(2,1)} %copy-done.2), channel_id=1, replica_groups=mesh['section'=2,'dp'=4,'tensor'=4] {'tensor'}, dimensions={1}, use_global_device_ids=true | all-gather | bytes 163840 | tf_op jit(solution)/shard_map/while/body/eval_jaxpr/all_gather | solution.py:100
  212.3 3.0 conditional.7
  220.8 7.4 %conditional.6 = (bf16[16,1024]{1,0:T(8,128)(2,1)S(1)}, f32[64,64]{1,0:T(8,128)}) conditional(s32[]{:T(128)} %convert_element_type.136, f32[64,64]{1,0:T(8,128)} %get-tuple-element.548, (bf16[16,4096]{1,0:T(8,128)(2,1)S(1)}, f32[128,4096]{1,0:T(8,128)S(1)}, s32[]{:T(128)}, bf16[1024,4096]{1,0:T(8,128)(2,1)}, bf16[128,64]{1,0:T(8,128)(2,1)}, ...), branch_computations={%region_3.3_spmd, %region_4.4_spmd} | conditional | flops 143152128 | bytes 10310676 | solution.py:94
  220.9 5.6 %convolution_convert_fusion = bf16[16,1024]{1,0:T(8,128)(2,1)S(1)} fusion(bf16[1024,4096]{1,0:T(8,128)(2,1)} %get-tuple-element.308, f32[128,4096]{1,0:T(8,128)S(1)} %get-tuple-element.306, s32[]{:T(128)} %get-tuple-element.307, bf16[16,4096]{1,0:T(8,128)(2,1)S(1)} %get-tuple-element.305), kind=kOutput, calls=%fused_computation.1 | convolution fusion | flops 134430720 | bytes 8814596 | tf_op jit(solution)/shard_map/while/body/eval_jaxpr/cond/branch_1_fun/dot_general | solution.py:75
  228.9 10.8 %all_gather.21 = bf16[16,4096]{1,0:T(8,128)(2,1)S(1)} all-gather(bf16[16,1024]{1,0:T(8,128)(2,1)} %copy-done.2), channel_id=1, replica_groups=mesh['section'=2,'dp'=4,'tensor'=4] {'tensor'}, dimensions={1}, use_global_device_ids=true | all-gather | bytes 163840 | tf_op jit(solution)/shard_map/while/body/eval_jaxpr/all_gather | solution.py:100
  239.6 3.0 conditional.7
  242.6 5.3 %collective-permute-start = (bf16[16,4096]{1,0:T(8,128)(2,1)S(1)}, bf16[16,4096]{1,0:T(8,128)(2,1)S(1)}, u32[]{:S(2)}, u32[]{:S(2)}) collective-permute-start(bf16[16,4096]{1,0:T(8,128)(2,1)S(1)} %get-tuple-element.588), channel_id=1, source_target_pairs={{16,0},{17,1},{18,2},{19,3},{20,4},{21,5},{22,6},{23,7},{24,8},{25... | collective-permute-start | bytes 393224 | tf_op jit(solution)/shard_map/while/body/eval_jaxpr/ppermute | solution.py:16
  252.2 7.4 %conditional.6 = (bf16[16,1024]{1,0:T(8,128)(2,1)S(1)}, f32[64,64]{1,0:T(8,128)}) conditional(s32[]{:T(128)} %convert_element_type.136, f32[64,64]{1,0:T(8,128)} %get-tuple-element.548, (bf16[16,4096]{1,0:T(8,128)(2,1)S(1)}, f32[128,4096]{1,0:T(8,128)S(1)}, s32[]{:T(128)}, bf16[1024,4096]{1,0:T(8,128)(2,1)}, bf16[128,64]{1,0:T(8,128)(2,1)}, ...), branch_computations={%region_3.3_spmd, %region_4.4_spmd} | conditional | flops 143152128 | bytes 10310676 | solution.py:94
  252.2 5.6 %convolution_convert_fusion = bf16[16,1024]{1,0:T(8,128)(2,1)S(1)} fusion(bf16[1024,4096]{1,0:T(8,128)(2,1)} %get-tuple-element.308, f32[128,4096]{1,0:T(8,128)S(1)} %get-tuple-element.306, s32[]{:T(128)} %get-tuple-element.307, bf16[16,4096]{1,0:T(8,128)(2,1)S(1)} %get-tuple-element.305), kind=kOutput, calls=%fused_computation.1 | convolution fusion | flops 134430720 | bytes 8814596 | tf_op jit(solution)/shard_map/while/body/eval_jaxpr/cond/branch_1_fun/dot_general | solution.py:75
  260.2 10.7 %all_gather.21 = bf16[16,4096]{1,0:T(8,128)(2,1)S(1)} all-gather(bf16[16,1024]{1,0:T(8,128)(2,1)} %copy-done.2), channel_id=1, replica_groups=mesh['section'=2,'dp'=4,'tensor'=4] {'tensor'}, dimensions={1}, use_global_device_ids=true | all-gather | bytes 163840 | tf_op jit(solution)/shard_map/while/body/eval_jaxpr/all_gather | solution.py:100
  270.9 3.0 conditional.7
  273.9 5.3 %collective-permute-start = (bf16[16,4096]{1,0:T(8,128)(2,1)S(1)}, bf16[16,4096]{1,0:T(8,128)(2,1)S(1)}, u32[]{:S(2)}, u32[]{:S(2)}) collective-permute-start(bf16[16,4096]{1,0:T(8,128)(2,1)S(1)} %get-tuple-element.588), channel_id=1, source_target_pairs={{16,0},{17,1},{18,2},{19,3},{20,4},{21,5},{22,6},{23,7},{24,8},{25... | collective-permute-start | bytes 393224 | tf_op jit(solution)/shard_map/while/body/eval_jaxpr/ppermute | solution.py:16
  283.5 7.4 %conditional.6 = (bf16[16,1024]{1,0:T(8,128)(2,1)S(1)}, f32[64,64]{1,0:T(8,128)}) conditional(s32[]{:T(128)} %convert_element_type.136, f32[64,64]{1,0:T(8,128)} %get-tuple-element.548, (bf16[16,4096]{1,0:T(8,128)(2,1)S(1)}, f32[128,4096]{1,0:T(8,128)S(1)}, s32[]{:T(128)}, bf16[1024,4096]{1,0:T(8,128)(2,1)}, bf16[128,64]{1,0:T(8,128)(2,1)}, ...), branch_computations={%region_3.3_spmd, %region_4.4_spmd} | conditional | flops 143152128 | bytes 10310676 | solution.py:94
  283.5 5.6 %convolution_convert_fusion = bf16[16,1024]{1,0:T(8,128)(2,1)S(1)} fusion(bf16[1024,4096]{1,0:T(8,128)(2,1)} %get-tuple-element.308, f32[128,4096]{1,0:T(8,128)S(1)} %get-tuple-element.306, s32[]{:T(128)} %get-tuple-element.307, bf16[16,4096]{1,0:T(8,128)(2,1)S(1)} %get-tuple-element.305), kind=kOutput, calls=%fused_computation.1 | convolution fusion | flops 134430720 | bytes 8814596 | tf_op jit(solution)/shard_map/while/body/eval_jaxpr/cond/branch_1_fun/dot_general | solution.py:75
  291.5 10.7 %all_gather.21 = bf16[16,4096]{1,0:T(8,128)(2,1)S(1)} all-gather(bf16[16,1024]{1,0:T(8,128)(2,1)} %copy-done.2), channel_id=1, replica_groups=mesh['section'=2,'dp'=4,'tensor'=4] {'tensor'}, dimensions={1}, use_global_device_ids=true | all-gather | bytes 163840 | tf_op jit(solution)/shard_map/while/body/eval_jaxpr/all_gather | solution.py:100
  302.2 3.0 conditional.7
  305.2 5.3 %collective-permute-start = (bf16[16,4096]{1,0:T(8,128)(2,1)S(1)}, bf16[16,4096]{1,0:T(8,128)(2,1)S(1)}, u32[]{:S(2)}, u32[]{:S(2)}) collective-permute-start(bf16[16,4096]{1,0:T(8,128)(2,1)S(1)} %get-tuple-element.588), channel_id=1, source_target_pairs={{16,0},{17,1},{18,2},{19,3},{20,4},{21,5},{22,6},{23,7},{24,8},{25... | collective-permute-start | bytes 393224 | tf_op jit(solution)/shard_map/while/body/eval_jaxpr/ppermute | solution.py:16
  314.7 7.4 %conditional.6 = (bf16[16,1024]{1,0:T(8,128)(2,1)S(1)}, f32[64,64]{1,0:T(8,128)}) conditional(s32[]{:T(128)} %convert_element_type.136, f32[64,64]{1,0:T(8,128)} %get-tuple-element.548, (bf16[16,4096]{1,0:T(8,128)(2,1)S(1)}, f32[128,4096]{1,0:T(8,128)S(1)}, s32[]{:T(128)}, bf16[1024,4096]{1,0:T(8,128)(2,1)}, bf16[128,64]{1,0:T(8,128)(2,1)}, ...), branch_computations={%region_3.3_spmd, %region_4.4_spmd} | conditional | flops 143152128 | bytes 10310676 | solution.py:94
  314.8 5.6 %convolution_convert_fusion = bf16[16,1024]{1,0:T(8,128)(2,1)S(1)} fusion(bf16[1024,4096]{1,0:T(8,128)(2,1)} %get-tuple-element.308, f32[128,4096]{1,0:T(8,128)S(1)} %get-tuple-element.306, s32[]{:T(128)} %get-tuple-element.307, bf16[16,4096]{1,0:T(8,128)(2,1)S(1)} %get-tuple-element.305), kind=kOutput, calls=%fused_computation.1 | convolution fusion | flops 134430720 | bytes 8814596 | tf_op jit(solution)/shard_map/while/body/eval_jaxpr/cond/branch_1_fun/dot_general | solution.py:75
  322.8 10.7 %all_gather.21 = bf16[16,4096]{1,0:T(8,128)(2,1)S(1)} all-gather(bf16[16,1024]{1,0:T(8,128)(2,1)} %copy-done.2), channel_id=1, replica_groups=mesh['section'=2,'dp'=4,'tensor'=4] {'tensor'}, dimensions={1}, use_global_device_ids=true | all-gather | bytes 163840 | tf_op jit(solution)/shard_map/while/body/eval_jaxpr/all_gather | solution.py:100
  333.5 3.0 conditional.7
  336.4 5.2 %collective-permute-start = (bf16[16,4096]{1,0:T(8,128)(2,1)S(1)}, bf16[16,4096]{1,0:T(8,128)(2,1)S(1)}, u32[]{:S(2)}, u32[]{:S(2)}) collective-permute-start(bf16[16,4096]{1,0:T(8,128)(2,1)S(1)} %get-tuple-element.588), channel_id=1, source_target_pairs={{16,0},{17,1},{18,2},{19,3},{20,4},{21,5},{22,6},{23,7},{24,8},{25... | collective-permute-start | bytes 393224 | tf_op jit(solution)/shard_map/while/body/eval_jaxpr/ppermute | solution.py:16
  345.9 7.4 %conditional.6 = (bf16[16,1024]{1,0:T(8,128)(2,1)S(1)}, f32[64,64]{1,0:T(8,128)}) conditional(s32[]{:T(128)} %convert_element_type.136, f32[64,64]{1,0:T(8,128)} %get-tuple-element.548, (bf16[16,4096]{1,0:T(8,128)(2,1)S(1)}, f32[128,4096]{1,0:T(8,128)S(1)}, s32[]{:T(128)}, bf16[1024,4096]{1,0:T(8,128)(2,1)}, bf16[128,64]{1,0:T(8,128)(2,1)}, ...), branch_computations={%region_3.3_spmd, %region_4.4_spmd} | conditional | flops 143152128 | bytes 10310676 | solution.py:94
  345.9 5.6 %convolution_convert_fusion = bf16[16,1024]{1,0:T(8,128)(2,1)S(1)} fusion(bf16[1024,4096]{1,0:T(8,128)(2,1)} %get-tuple-element.308, f32[128,4096]{1,0:T(8,128)S(1)} %get-tuple-element.306, s32[]{:T(128)} %get-tuple-element.307, bf16[16,4096]{1,0:T(8,128)(2,1)S(1)} %get-tuple-element.305), kind=kOutput, calls=%fused_computation.1 | convolution fusion | flops 134430720 | bytes 8814596 | tf_op jit(solution)/shard_map/while/body/eval_jaxpr/cond/branch_1_fun/dot_general | solution.py:75
  354.0 10.7 %all_gather.21 = bf16[16,4096]{1,0:T(8,128)(2,1)S(1)} all-gather(bf16[16,1024]{1,0:T(8,128)(2,1)} %copy-done.2), channel_id=1, replica_groups=mesh['section'=2,'dp'=4,'tensor'=4] {'tensor'}, dimensions={1}, use_global_device_ids=true | all-gather | bytes 163840 | tf_op jit(solution)/shard_map/while/body/eval_jaxpr/all_gather | solution.py:100
  364.7 3.0 conditional.7
  367.6 5.3 %collective-permute-start = (bf16[16,4096]{1,0:T(8,128)(2,1)S(1)}, bf16[16,4096]{1,0:T(8,128)(2,1)S(1)}, u32[]{:S(2)}, u32[]{:S(2)}) collective-permute-start(bf16[16,4096]{1,0:T(8,128)(2,1)S(1)} %get-tuple-element.588), channel_id=1, source_target_pairs={{16,0},{17,1},{18,2},{19,3},{20,4},{21,5},{22,6},{23,7},{24,8},{25... | collective-permute-start | bytes 393224 | tf_op jit(solution)/shard_map/while/body/eval_jaxpr/ppermute | solution.py:16
  377.2 7.4 %conditional.6 = (bf16[16,1024]{1,0:T(8,128)(2,1)S(1)}, f32[64,64]{1,0:T(8,128)}) conditional(s32[]{:T(128)} %convert_element_type.136, f32[64,64]{1,0:T(8,128)} %get-tuple-element.548, (bf16[16,4096]{1,0:T(8,128)(2,1)S(1)}, f32[128,4096]{1,0:T(8,128)S(1)}, s32[]{:T(128)}, bf16[1024,4096]{1,0:T(8,128)(2,1)}, bf16[128,64]{1,0:T(8,128)(2,1)}, ...), branch_computations={%region_3.3_spmd, %region_4.4_spmd} | conditional | flops 143152128 | bytes 10310676 | solution.py:94
  377.2 5.6 %convolution_convert_fusion = bf16[16,1024]{1,0:T(8,128)(2,1)S(1)} fusion(bf16[1024,4096]{1,0:T(8,128)(2,1)} %get-tuple-element.308, f32[128,4096]{1,0:T(8,128)S(1)} %get-tuple-element.306, s32[]{:T(128)} %get-tuple-element.307, bf16[16,4096]{1,0:T(8,128)(2,1)S(1)} %get-tuple-element.305), kind=kOutput, calls=%fused_computation.1 | convolution fusion | flops 134430720 | bytes 8814596 | tf_op jit(solution)/shard_map/while/body/eval_jaxpr/cond/branch_1_fun/dot_general | solution.py:75
  385.2 10.7 %all_gather.21 = bf16[16,4096]{1,0:T(8,128)(2,1)S(1)} all-gather(bf16[16,1024]{1,0:T(8,128)(2,1)} %copy-done.2), channel_id=1, replica_groups=mesh['section'=2,'dp'=4,'tensor'=4] {'tensor'}, dimensions={1}, use_global_device_ids=true | all-gather | bytes 163840 | tf_op jit(solution)/shard_map/while/body/eval_jaxpr/all_gather | solution.py:100
  395.9 3.0 conditional.7
  398.9 5.2 %collective-permute-start = (bf16[16,4096]{1,0:T(8,128)(2,1)S(1)}, bf16[16,4096]{1,0:T(8,128)(2,1)S(1)}, u32[]{:S(2)}, u32[]{:S(2)}) collective-permute-start(bf16[16,4096]{1,0:T(8,128)(2,1)S(1)} %get-tuple-element.588), channel_id=1, source_target_pairs={{16,0},{17,1},{18,2},{19,3},{20,4},{21,5},{22,6},{23,7},{24,8},{25... | collective-permute-start | bytes 393224 | tf_op jit(solution)/shard_map/while/body/eval_jaxpr/ppermute | solution.py:16
  408.4 7.4 %conditional.6 = (bf16[16,1024]{1,0:T(8,128)(2,1)S(1)}, f32[64,64]{1,0:T(8,128)}) conditional(s32[]{:T(128)} %convert_element_type.136, f32[64,64]{1,0:T(8,128)} %get-tuple-element.548, (bf16[16,4096]{1,0:T(8,128)(2,1)S(1)}, f32[128,4096]{1,0:T(8,128)S(1)}, s32[]{:T(128)}, bf16[1024,4096]{1,0:T(8,128)(2,1)}, bf16[128,64]{1,0:T(8,128)(2,1)}, ...), branch_computations={%region_3.3_spmd, %region_4.4_spmd} | conditional | flops 143152128 | bytes 10310676 | solution.py:94
  408.4 5.6 %convolution_convert_fusion = bf16[16,1024]{1,0:T(8,128)(2,1)S(1)} fusion(bf16[1024,4096]{1,0:T(8,128)(2,1)} %get-tuple-element.308, f32[128,4096]{1,0:T(8,128)S(1)} %get-tuple-element.306, s32[]{:T(128)} %get-tuple-element.307, bf16[16,4096]{1,0:T(8,128)(2,1)S(1)} %get-tuple-element.305), kind=kOutput, calls=%fused_computation.1 | convolution fusion | flops 134430720 | bytes 8814596 | tf_op jit(solution)/shard_map/while/body/eval_jaxpr/cond/branch_1_fun/dot_general | solution.py:75
  416.4 10.7 %all_gather.21 = bf16[16,4096]{1,0:T(8,128)(2,1)S(1)} all-gather(bf16[16,1024]{1,0:T(8,128)(2,1)} %copy-done.2), channel_id=1, replica_groups=mesh['section'=2,'dp'=4,'tensor'=4] {'tensor'}, dimensions={1}, use_global_device_ids=true | all-gather | bytes 163840 | tf_op jit(solution)/shard_map/while/body/eval_jaxpr/all_gather | solution.py:100
  427.1 2.9 conditional.7
  430.0 5.4 %collective-permute-start = (bf16[16,4096]{1,0:T(8,128)(2,1)S(1)}, bf16[16,4096]{1,0:T(8,128)(2,1)S(1)}, u32[]{:S(2)}, u32[]{:S(2)}) collective-permute-start(bf16[16,4096]{1,0:T(8,128)(2,1)S(1)} %get-tuple-element.588), channel_id=1, source_target_pairs={{16,0},{17,1},{18,2},{19,3},{20,4},{21,5},{22,6},{23,7},{24,8},{25... | collective-permute-start | bytes 393224 | tf_op jit(solution)/shard_map/while/body/eval_jaxpr/ppermute | solution.py:16
  440.3 10.8 %all_gather.21 = bf16[16,4096]{1,0:T(8,128)(2,1)S(1)} all-gather(bf16[16,1024]{1,0:T(8,128)(2,1)} %copy-done.2), channel_id=1, replica_groups=mesh['section'=2,'dp'=4,'tensor'=4] {'tensor'}, dimensions={1}, use_global_device_ids=true | all-gather | bytes 163840 | tf_op jit(solution)/shard_map/while/body/eval_jaxpr/all_gather | solution.py:100
  451.1 15.3 %collective-permute-start = (bf16[16,4096]{1,0:T(8,128)(2,1)S(1)}, bf16[16,4096]{1,0:T(8,128)(2,1)S(1)}, u32[]{:S(2)}, u32[]{:S(2)}) collective-permute-start(bf16[16,4096]{1,0:T(8,128)(2,1)S(1)} %get-tuple-element.588), channel_id=1, source_target_pairs={{16,0},{17,1},{18,2},{19,3},{20,4},{21,5},{22,6},{23,7},{24,8},{25... | collective-permute-start | bytes 393224 | tf_op jit(solution)/shard_map/while/body/eval_jaxpr/ppermute | solution.py:16
  468.8 8.0 %psum.14 = f32[2,1024]{1,0:T(2,128)S(1)} all-reduce(f32[2,1024]{1,0:T(2,128)S(1)} %broadcast_multiply_fusion.1), channel_id=1, replica_groups=mesh['section'=2,'dp'=4,'tensor'=4] {'dp'}, use_global_device_ids=true, to_apply=%region_9.10 | all-reduce | flops 2048 | bytes 16384 | tf_op jit(solution)/shard_map/psum | solution.py:130
  477.0 17.0 %psum.15 = f32[2,64]{1,0:T(2,128)} all-reduce(f32[2,64]{1,0:T(2,128)S(1)} %fusion.32), channel_id=1, replica_groups=mesh['section'=2,'dp'=4,'tensor'=4] {'section','tensor'}, use_global_device_ids=true, to_apply=%region_10.11 | all-reduce | flops 128 | bytes 1024 | tf_op jit(solution)/shard_map/psum | solution.py:133
  (124 shorter events, 92.8 us)
Async XLA Ops:
  7.2 469.7 %copy-start = (bf16[1,64,1024]{2,1,0:T(8,128)(2,1)S(1)}, bf16[1,64,1024]{2,1,0:T(8,128)(2,1)}, u32[]{:S(2)}) copy-start(bf16[1,64,1024]{2,1,0:T(8,128)(2,1)} %param.17) | copy-start | bytes 393220
  7.2 1.3 copy-start.1
  7.2 2.1 copy-start.3
  7.2 92.1 %all-gather.5.cloned.1.call-start = ((), (), s32[]{:S(2)}) async-start(), calls=%async_computation | async-start | bytes 10485760 | tf_op jit(solution)/shard_map/all_gather | solution.py:52
  7.9 177.9 %all-gather.7.cloned.1.call-start = ((), (), s32[]{:S(2)}) async-start(), calls=%async_computation.1 | async-start | bytes 5242880 | tf_op jit(solution)/shard_map/all_gather | solution.py:56
  99.3 5.7 %copy-start.7 = (s32[1,2]{1,0:T(1,128)S(1)}, s32[1,2]{1,0:T(1,128)}, u32[]{:S(2)}) copy-start(s32[1,2]{1,0:T(1,128)} %param.15) | copy-start | bytes 28
  106.8 1.4 copy-start.6
  106.8 1.4 copy-start.4
  201.0 0.6 copy-start.2
  215.3 2.3 collective-permute-start
  228.3 0.6 copy-start.2
  242.6 6.3 %collective-permute-start = (bf16[16,4096]{1,0:T(8,128)(2,1)S(1)}, bf16[16,4096]{1,0:T(8,128)(2,1)S(1)}, u32[]{:S(2)}, u32[]{:S(2)}) collective-permute-start(bf16[16,4096]{1,0:T(8,128)(2,1)S(1)} %get-tuple-element.588), channel_id=1, source_target_pairs={{16,0},{17,1},{18,2},{19,3},{20,4},{21,5},{22,6},{23,7},{24,8},{25... | collective-permute-start | bytes 393224 | tf_op jit(solution)/shard_map/while/body/eval_jaxpr/ppermute | solution.py:16
  259.6 0.6 copy-start.2
  273.9 6.2 %collective-permute-start = (bf16[16,4096]{1,0:T(8,128)(2,1)S(1)}, bf16[16,4096]{1,0:T(8,128)(2,1)S(1)}, u32[]{:S(2)}, u32[]{:S(2)}) collective-permute-start(bf16[16,4096]{1,0:T(8,128)(2,1)S(1)} %get-tuple-element.588), channel_id=1, source_target_pairs={{16,0},{17,1},{18,2},{19,3},{20,4},{21,5},{22,6},{23,7},{24,8},{25... | collective-permute-start | bytes 393224 | tf_op jit(solution)/shard_map/while/body/eval_jaxpr/ppermute | solution.py:16
  290.9 0.6 copy-start.2
  305.2 6.2 %collective-permute-start = (bf16[16,4096]{1,0:T(8,128)(2,1)S(1)}, bf16[16,4096]{1,0:T(8,128)(2,1)S(1)}, u32[]{:S(2)}, u32[]{:S(2)}) collective-permute-start(bf16[16,4096]{1,0:T(8,128)(2,1)S(1)} %get-tuple-element.588), channel_id=1, source_target_pairs={{16,0},{17,1},{18,2},{19,3},{20,4},{21,5},{22,6},{23,7},{24,8},{25... | collective-permute-start | bytes 393224 | tf_op jit(solution)/shard_map/while/body/eval_jaxpr/ppermute | solution.py:16
  322.2 0.6 copy-start.2
  336.4 6.2 %collective-permute-start = (bf16[16,4096]{1,0:T(8,128)(2,1)S(1)}, bf16[16,4096]{1,0:T(8,128)(2,1)S(1)}, u32[]{:S(2)}, u32[]{:S(2)}) collective-permute-start(bf16[16,4096]{1,0:T(8,128)(2,1)S(1)} %get-tuple-element.588), channel_id=1, source_target_pairs={{16,0},{17,1},{18,2},{19,3},{20,4},{21,5},{22,6},{23,7},{24,8},{25... | collective-permute-start | bytes 393224 | tf_op jit(solution)/shard_map/while/body/eval_jaxpr/ppermute | solution.py:16
  353.4 0.6 copy-start.2
  367.6 6.2 %collective-permute-start = (bf16[16,4096]{1,0:T(8,128)(2,1)S(1)}, bf16[16,4096]{1,0:T(8,128)(2,1)S(1)}, u32[]{:S(2)}, u32[]{:S(2)}) collective-permute-start(bf16[16,4096]{1,0:T(8,128)(2,1)S(1)} %get-tuple-element.588), channel_id=1, source_target_pairs={{16,0},{17,1},{18,2},{19,3},{20,4},{21,5},{22,6},{23,7},{24,8},{25... | collective-permute-start | bytes 393224 | tf_op jit(solution)/shard_map/while/body/eval_jaxpr/ppermute | solution.py:16
  384.6 0.6 copy-start.2
  398.9 6.2 %collective-permute-start = (bf16[16,4096]{1,0:T(8,128)(2,1)S(1)}, bf16[16,4096]{1,0:T(8,128)(2,1)S(1)}, u32[]{:S(2)}, u32[]{:S(2)}) collective-permute-start(bf16[16,4096]{1,0:T(8,128)(2,1)S(1)} %get-tuple-element.588), channel_id=1, source_target_pairs={{16,0},{17,1},{18,2},{19,3},{20,4},{21,5},{22,6},{23,7},{24,8},{25... | collective-permute-start | bytes 393224 | tf_op jit(solution)/shard_map/while/body/eval_jaxpr/ppermute | solution.py:16
  415.8 0.6 copy-start.2
  430.0 6.3 %collective-permute-start = (bf16[16,4096]{1,0:T(8,128)(2,1)S(1)}, bf16[16,4096]{1,0:T(8,128)(2,1)S(1)}, u32[]{:S(2)}, u32[]{:S(2)}) collective-permute-start(bf16[16,4096]{1,0:T(8,128)(2,1)S(1)} %get-tuple-element.588), channel_id=1, source_target_pairs={{16,0},{17,1},{18,2},{19,3},{20,4},{21,5},{22,6},{23,7},{24,8},{25... | collective-permute-start | bytes 393224 | tf_op jit(solution)/shard_map/while/body/eval_jaxpr/ppermute | solution.py:16
  439.7 0.6 copy-start.2
  451.1 16.3 %collective-permute-start = (bf16[16,4096]{1,0:T(8,128)(2,1)S(1)}, bf16[16,4096]{1,0:T(8,128)(2,1)S(1)}, u32[]{:S(2)}, u32[]{:S(2)}) collective-permute-start(bf16[16,4096]{1,0:T(8,128)(2,1)S(1)} %get-tuple-element.588), channel_id=1, source_target_pairs={{16,0},{17,1},{18,2},{19,3},{20,4},{21,5},{22,6},{23,7},{24,8},{25... | collective-permute-start | bytes 393224 | tf_op jit(solution)/shard_map/while/body/eval_jaxpr/ppermute | solution.py:16
  476.9 17.2 %copy-start.5 = (f32[2,1024]{1,0:T(2,128)}, f32[2,1024]{1,0:T(2,128)S(1)}, u32[]{:S(2)}) copy-start(f32[2,1024]{1,0:T(2,128)S(1)} %psum.14) | copy-start | bytes 24580
Sparse Core Ops, SparseCore 0:
  9.9 89.3 all-gather.4
  105.1 80.7 all-gather.6
